TPU v7x, 32 devices: a whole 2x2x4 slice. The times are simulated.
32 devices in a mesh: sec: 8 (over y, x, core), ch: 4 (over z).
Axes of the slice: x: 2, y: 2, z: 4, core: 2. Of those that a mesh axis runs over, the one named last changes fastest.
Arguments:
- start_amps: bfloat16 [6, 1024, 2048], P(None, 'ch'), may hold values from -6 to 6
- energies: float32 [6], replicated, may hold values from 0.5 to 2
- thresholds: bfloat16 [8, 1024], P('sec', 'ch'), may hold values from -3 to -1
- intersection: bfloat16 [8, 1024, 1024], P('sec', 'ch'), may hold values from -0.2 to 1
Outputs:
- boundary_amps: bfloat16 [8, 6, 1024, 2048], P('sec', None, 'ch')
All inputs are finite; a program needn't handle non-finite values.
Results may differ from a plain program's by a relative error of at most 0.04.
Values may be sent and summed in bfloat16 or wider, within the bound.
A program may use at most 64 MiB of HBM per device.

v0:
```python
import jax
import jax.numpy as jnp
from jax import lax
from jax.sharding import PartitionSpec as P


def passed_along(value, axis, steps):
    count = lax.axis_size(axis)
    leading, last = (max(0, -steps), min(count, count - steps))
    return lax.ppermute(value, axis, [(source, source + steps) for source in range(leading, last)])


def per_device(start_amps, energies, thresholds, intersection):
    sectors = lax.axis_size("sec")
    sector_index = lax.axis_index("sec")
    groups = lax.axis_size("ch")
    energy_count = energies.shape[0]
    step_count = sectors + energy_count - 1
    row_count = intersection.shape[1]
    width_cols = start_amps.shape[2]
    half_cols = width_cols // 2
    col_width = half_cols // groups
    intersection_whole, thresholds_whole = (
        lax.all_gather(intersection, "ch", axis=1, tiled=True),
        lax.all_gather(thresholds, "ch", axis=1, tiled=True),
    )
    basis_change = intersection_whole[0]
    channel_thresholds = thresholds_whole[0].astype(jnp.float32)
    channel_count = basis_change.shape[0]
    paired = start_amps.reshape(energy_count, row_count, 2, half_cols)
    start_cols = lax.all_to_all(paired, "ch", split_axis=3, concat_axis=1, tiled=True)
    stored_init = jnp.zeros((energy_count, channel_count, 2, col_width), jnp.bfloat16)

    def multiply(flat):
        return jnp.dot(basis_change, flat, preferred_element_type=jnp.float32).astype(jnp.bfloat16)

    def skipped(flat):
        return jnp.zeros((channel_count, 2 * col_width), jnp.bfloat16)

    def step(step_index, state_pair):
        outgoing, stored = state_pair
        incoming = passed_along(outgoing, "sec", 1)
        energy_raw = step_index - sector_index
        active = (energy_raw >= 0) & (energy_raw < energy_count)
        energy_slot = jnp.clip(energy_raw, 0, energy_count - 1)
        initial = lax.dynamic_index_in_dim(start_cols, energy_slot, 0, keepdims=False)
        source = jnp.where(sector_index == 0, initial, incoming).astype(jnp.float32)
        wavenumber = jnp.sqrt(energies[energy_slot] - channel_thresholds)[:, None]
        values_part = source[:, 0, :]
        slopes_part = source[:, 1, :]
        cosine = jnp.cos(wavenumber)
        sine_term = jnp.sin(wavenumber)
        new_values = cosine * values_part + sine_term / wavenumber * slopes_part
        new_slopes = -wavenumber * sine_term * values_part + cosine * slopes_part
        rotated = jnp.stack([new_values, new_slopes], axis=1).astype(jnp.bfloat16)
        flat = rotated.reshape(channel_count, 2 * col_width)
        fresh = lax.cond(active, multiply, skipped, flat)
        fresh = fresh.reshape(channel_count, 2, col_width)
        previous = lax.dynamic_index_in_dim(stored, energy_slot, 0, keepdims=False)
        kept = jnp.where(active, fresh, previous)
        stored = lax.dynamic_update_index_in_dim(stored, kept, energy_slot, 0)
        return (fresh, stored)

    outgoing_init = jnp.zeros((channel_count, 2, col_width), jnp.bfloat16)
    final_pair = lax.fori_loop(0, step_count, step, (outgoing_init, stored_init))
    returned = lax.all_to_all(final_pair[1], "ch", split_axis=1, concat_axis=3, tiled=True)
    return returned.reshape(energy_count, row_count, width_cols)[None]


def solution(mesh):
    in_specs = (P(None, "ch", None), P(), P("sec", "ch"), P("sec", "ch", None))
    out_specs = P("sec", None, "ch", None)
    return jax.shard_map(
        per_device, mesh=mesh, in_specs=in_specs, out_specs=out_specs, check_vma=False
    )
```

profile of v0, /device:TPU:4, one launch (start us, length us, event | category | flops | bytes accessed | tf_op | source)
XLA Modules:
  0.0 743.5 jit_solution(3226323656198132357)
XLA Ops:
  6.5 8.6 %copy.31 = bf16[6,256,2048]{1,2,0:T(8,128)(2,1)} copy(bf16[6,256,2048]{2,1,0:T(8,128)(2,1)} %param.8) | data formatting | bytes 12582912 | tf_op args[0]
  15.1 12.7 %copy.32 = bf16[6,256,2,1024]{1,2,0,3:T(2,128)(2,1)} copy(bf16[6,256,2,1024]{1,3,2,0:T(8,128)(2,1)} %bitcast.29) | data formatting | bytes 12582912 | tf_op jit(solution)/shard_map/reshape | solution.py:30
  27.9 5.4 all-to-all-start
  34.0 140.4 %all_gather.6 = bf16[1,1024]{1,0:T(2,128)(2,1)S(1)} all-gather(bf16[1,256]{1,0:T(2,128)(2,1)S(1)} %copy-done), channel_id=1, replica_groups=mesh['sec'=8,'ch'=4] {'ch'}, dimensions={1}, use_global_device_ids=true | all-gather | bytes 2560 | tf_op jit(solution)/shard_map/all_gather | solution.py:25
  174.4 31.1 %all-to-all-done = bf16[6,256,2,1024]{1,2,0,3:T(2,128)(2,1)} async-done(((bf16[6,256,2,1024]{1,2,0,3:T(2,128)(2,1)}), bf16[6,256,2,1024]{1,2,0,3:T(2,128)(2,1)}, u32[]{:S(2)}, u32[]{:S(2)}) %all-to-all-start) | async-done | bytes 6291488 | tf_op jit(solution)/shard_map/all_to_all | solution.py:31
  205.4 6.4 copy.33
  211.9 8.6 %copy.34 = bf16[6,4,256,2,256]{4,2,1,3,0:T(8,128)(2,1)} copy(bf16[6,4,256,2,256]{2,4,1,3,0:T(8,128)(2,1)} %bitcast.27) | data formatting | bytes 12582912 | tf_op jit(solution)/shard_map/all_to_all | solution.py:31
  221.6 5.9 broadcast_in_dim.14.clone
  227.6 353.1 %while.16 = (s32[]{:T(128)}, bf16[1024,2,256]{0,2,1:T(8,128)(2,1)}, bf16[6,1024,2,256]{3,2,0,1:T(2,128)(2,1)}, s32[]{:T(128)}, f32[6]{0:T(128)S(1)}, /*index=5*/...) while((s32[]{:T(128)}, bf16[1024,2,256]{0,2,1:T(8,128)(2,1)}, ...), condition=%wide.region_3.4_spmd, body=%wide.region_0.3_spmd.sunk | while | flops 1078464512 | bytes 46166332 | solution.py:65
  227.6 2.2 copy.45
  236.7 10.3 %collective-permute-done = bf16[1024,2,256]{2,0,1:T(8,128)(2,1)S(1)} collective-permute-done((bf16[1024,2,256]{2,0,1:T(8,128)(2,1)}, bf16[1024,2,256]{2,0,1:T(8,128)(2,1)S(1)}, u32[]{:S(2)}, u32[]{:S(2)}) %collective-permute-start) | collective-permute-done | bytes 1048608 | tf_op jit(solution)/shard_map/while/body/eval_jaxpr/ppermute | solution.py:10
  253.0 2.2 copy.45
  262.2 10.3 %collective-permute-done = bf16[1024,2,256]{2,0,1:T(8,128)(2,1)S(1)} collective-permute-done((bf16[1024,2,256]{2,0,1:T(8,128)(2,1)}, bf16[1024,2,256]{2,0,1:T(8,128)(2,1)S(1)}, u32[]{:S(2)}, u32[]{:S(2)}) %collective-permute-start) | collective-permute-done | bytes 1048608 | tf_op jit(solution)/shard_map/while/body/eval_jaxpr/ppermute | solution.py:10
  278.5 2.2 copy.45
  287.7 10.3 %collective-permute-done = bf16[1024,2,256]{2,0,1:T(8,128)(2,1)S(1)} collective-permute-done((bf16[1024,2,256]{2,0,1:T(8,128)(2,1)}, bf16[1024,2,256]{2,0,1:T(8,128)(2,1)S(1)}, u32[]{:S(2)}, u32[]{:S(2)}) %collective-permute-start) | collective-permute-done | bytes 1048608 | tf_op jit(solution)/shard_map/while/body/eval_jaxpr/ppermute | solution.py:10
  304.0 2.2 copy.45
  313.1 10.3 %collective-permute-done = bf16[1024,2,256]{2,0,1:T(8,128)(2,1)S(1)} collective-permute-done((bf16[1024,2,256]{2,0,1:T(8,128)(2,1)}, bf16[1024,2,256]{2,0,1:T(8,128)(2,1)S(1)}, u32[]{:S(2)}, u32[]{:S(2)}) %collective-permute-start) | collective-permute-done | bytes 1048608 | tf_op jit(solution)/shard_map/while/body/eval_jaxpr/ppermute | solution.py:10
  329.4 2.2 copy.45
  338.6 10.7 %collective-permute-done = bf16[1024,2,256]{2,0,1:T(8,128)(2,1)S(1)} collective-permute-done((bf16[1024,2,256]{2,0,1:T(8,128)(2,1)}, bf16[1024,2,256]{2,0,1:T(8,128)(2,1)S(1)}, u32[]{:S(2)}, u32[]{:S(2)}) %collective-permute-start) | collective-permute-done | bytes 1048608 | tf_op jit(solution)/shard_map/while/body/eval_jaxpr/ppermute | solution.py:10
  351.2 4.9 conditional.2
  352.6 2.3 convolution_convert_fusion
  358.9 2.2 copy.45
  368.0 10.3 %collective-permute-done = bf16[1024,2,256]{2,0,1:T(8,128)(2,1)S(1)} collective-permute-done((bf16[1024,2,256]{2,0,1:T(8,128)(2,1)}, bf16[1024,2,256]{2,0,1:T(8,128)(2,1)S(1)}, u32[]{:S(2)}, u32[]{:S(2)}) %collective-permute-start) | collective-permute-done | bytes 1048608 | tf_op jit(solution)/shard_map/while/body/eval_jaxpr/ppermute | solution.py:10
  380.3 4.9 conditional.2
  381.6 2.3 convolution_convert_fusion
  387.9 2.2 copy.45
  397.1 10.3 %collective-permute-done = bf16[1024,2,256]{2,0,1:T(8,128)(2,1)S(1)} collective-permute-done((bf16[1024,2,256]{2,0,1:T(8,128)(2,1)}, bf16[1024,2,256]{2,0,1:T(8,128)(2,1)S(1)}, u32[]{:S(2)}, u32[]{:S(2)}) %collective-permute-start) | collective-permute-done | bytes 1048608 | tf_op jit(solution)/shard_map/while/body/eval_jaxpr/ppermute | solution.py:10
  409.4 4.9 conditional.2
  410.7 2.3 convolution_convert_fusion
  417.0 2.2 copy.45
  426.2 10.3 %collective-permute-done = bf16[1024,2,256]{2,0,1:T(8,128)(2,1)S(1)} collective-permute-done((bf16[1024,2,256]{2,0,1:T(8,128)(2,1)}, bf16[1024,2,256]{2,0,1:T(8,128)(2,1)S(1)}, u32[]{:S(2)}, u32[]{:S(2)}) %collective-permute-start) | collective-permute-done | bytes 1048608 | tf_op jit(solution)/shard_map/while/body/eval_jaxpr/ppermute | solution.py:10
  438.4 4.9 conditional.2
  439.8 2.3 convolution_convert_fusion
  446.1 2.2 copy.45
  455.2 10.3 %collective-permute-done = bf16[1024,2,256]{2,0,1:T(8,128)(2,1)S(1)} collective-permute-done((bf16[1024,2,256]{2,0,1:T(8,128)(2,1)}, bf16[1024,2,256]{2,0,1:T(8,128)(2,1)S(1)}, u32[]{:S(2)}, u32[]{:S(2)}) %collective-permute-start) | collective-permute-done | bytes 1048608 | tf_op jit(solution)/shard_map/while/body/eval_jaxpr/ppermute | solution.py:10
  467.5 4.9 conditional.2
  468.9 2.3 convolution_convert_fusion
  475.2 2.2 copy.45
  484.3 10.3 %collective-permute-done = bf16[1024,2,256]{2,0,1:T(8,128)(2,1)S(1)} collective-permute-done((bf16[1024,2,256]{2,0,1:T(8,128)(2,1)}, bf16[1024,2,256]{2,0,1:T(8,128)(2,1)S(1)}, u32[]{:S(2)}, u32[]{:S(2)}) %collective-permute-start) | collective-permute-done | bytes 1048608 | tf_op jit(solution)/shard_map/while/body/eval_jaxpr/ppermute | solution.py:10
  496.6 4.9 conditional.2
  498.0 2.3 convolution_convert_fusion
  513.4 10.3 %collective-permute-done = bf16[1024,2,256]{2,0,1:T(8,128)(2,1)S(1)} collective-permute-done((bf16[1024,2,256]{2,0,1:T(8,128)(2,1)}, bf16[1024,2,256]{2,0,1:T(8,128)(2,1)S(1)}, u32[]{:S(2)}, u32[]{:S(2)}) %collective-permute-start) | collective-permute-done | bytes 1048608 | tf_op jit(solution)/shard_map/while/body/eval_jaxpr/ppermute | solution.py:10
  538.9 10.3 %collective-permute-done = bf16[1024,2,256]{2,0,1:T(8,128)(2,1)S(1)} collective-permute-done((bf16[1024,2,256]{2,0,1:T(8,128)(2,1)}, bf16[1024,2,256]{2,0,1:T(8,128)(2,1)S(1)}, u32[]{:S(2)}, u32[]{:S(2)}) %collective-permute-start) | collective-permute-done | bytes 1048608 | tf_op jit(solution)/shard_map/while/body/eval_jaxpr/ppermute | solution.py:10
  555.2 2.2 copy.45
  564.3 10.3 %collective-permute-done = bf16[1024,2,256]{2,0,1:T(8,128)(2,1)S(1)} collective-permute-done((bf16[1024,2,256]{2,0,1:T(8,128)(2,1)}, bf16[1024,2,256]{2,0,1:T(8,128)(2,1)S(1)}, u32[]{:S(2)}, u32[]{:S(2)}) %collective-permute-start) | collective-permute-done | bytes 1048608 | tf_op jit(solution)/shard_map/while/body/eval_jaxpr/ppermute | solution.py:10
  580.6 134.3 %all_to_all.33 = bf16[6,1024,2,256]{3,2,0,1:T(2,128)(2,1)S(1)} all-to-all(bf16[6,1024,2,256]{3,2,0,1:T(2,128)(2,1)} %get-tuple-element.205), channel_id=1, replica_groups=mesh['sec'=8,'ch'=4] {'ch'}, dimensions={1} | all-to-all | bytes 12582912 | tf_op jit(solution)/shard_map/all_to_all | solution.py:66
  714.9 10.7 %copy.36 = bf16[6,256,2,4,256]{4,3,2,1,0:T(4,128)(2,1)} copy(bf16[6,256,2,4,256]{4,2,0,1,3:T(2,128)(2,1)S(1)} %bitcast.28) | data formatting | bytes 12582912 | tf_op jit(solution)/shard_map/all_to_all | solution.py:66
  725.6 11.0 %broadcast_in_dim_reshape.3 = bf16[1,6,256,2048]{3,2,1,0:T(8,128)(2,1)} reshape(bf16[6,256,2,4,256]{4,3,2,1,0:T(4,128)(2,1)} %copy.36) | data formatting | bytes 12582912 | tf_op jit(solution)/shard_map/broadcast_in_dim;reshape | solution.py:67
  (219 shorter events, 189.4 us)
Async XLA Ops:
  27.9 6.1 copy-start
  27.9 177.6 %all-to-all-start = ((bf16[6,256,2,1024]{1,2,0,3:T(2,128)(2,1)}), bf16[6,256,2,1024]{1,2,0,3:T(2,128)(2,1)}, u32[]{:S(2)}, u32[]{:S(2)}) async-start(bf16[6,256,2,1024]{1,2,0,3:T(2,128)(2,1)} %copy.32), calls=%async_computation | async-start | bytes 12582912 | tf_op jit(solution)/shard_map/all_to_all | solution.py:31
  33.3 187.2 %all-gather.2.cloned.1.call-start = ((), (), s32[]{:S(2)}) async-start(), calls=%async_computation.2 | async-start | bytes 2621440 | tf_op jit(solution)/shard_map/all_gather | solution.py:24
  220.5 7.1 copy-start.2
  229.8 17.2 %collective-permute-start = (bf16[1024,2,256]{2,0,1:T(8,128)(2,1)}, bf16[1024,2,256]{2,0,1:T(8,128)(2,1)S(1)}, u32[]{:S(2)}, u32[]{:S(2)}) collective-permute-start(bf16[1024,2,256]{2,0,1:T(8,128)(2,1)} %copy.45), channel_id=1, source_target_pairs={{0,4},{4,8},{8,12},{12,16},{16,20},{20,24},{24,28},{1,5},{5,9},{9,... | collective-permute-start | bytes 3145736 | tf_op jit(solution)/shard_map/while/body/eval_jaxpr/ppermute | solution.py:10
  235.8 13.2 %copy-start.1 = (bf16[1024,1024]{1,0:T(8,128)(2,1)S(1)}, bf16[1024,1024]{1,0:T(8,128)(2,1)}, u32[]{:S(2)}) copy-start(bf16[1024,1024]{1,0:T(8,128)(2,1)} %get-tuple-element.365) | copy-start | bytes 6291460 | tf_op jit(solution)/shard_map/while
  255.3 17.2 %collective-permute-start = (bf16[1024,2,256]{2,0,1:T(8,128)(2,1)}, bf16[1024,2,256]{2,0,1:T(8,128)(2,1)S(1)}, u32[]{:S(2)}, u32[]{:S(2)}) collective-permute-start(bf16[1024,2,256]{2,0,1:T(8,128)(2,1)} %copy.45), channel_id=1, source_target_pairs={{0,4},{4,8},{8,12},{12,16},{16,20},{20,24},{24,28},{1,5},{5,9},{9,... | collective-permute-start | bytes 3145736 | tf_op jit(solution)/shard_map/while/body/eval_jaxpr/ppermute | solution.py:10
  261.3 13.2 %copy-start.1 = (bf16[1024,1024]{1,0:T(8,128)(2,1)S(1)}, bf16[1024,1024]{1,0:T(8,128)(2,1)}, u32[]{:S(2)}) copy-start(bf16[1024,1024]{1,0:T(8,128)(2,1)} %get-tuple-element.365) | copy-start | bytes 6291460 | tf_op jit(solution)/shard_map/while
  280.7 17.2 %collective-permute-start = (bf16[1024,2,256]{2,0,1:T(8,128)(2,1)}, bf16[1024,2,256]{2,0,1:T(8,128)(2,1)S(1)}, u32[]{:S(2)}, u32[]{:S(2)}) collective-permute-start(bf16[1024,2,256]{2,0,1:T(8,128)(2,1)} %copy.45), channel_id=1, source_target_pairs={{0,4},{4,8},{8,12},{12,16},{16,20},{20,24},{24,28},{1,5},{5,9},{9,... | collective-permute-start | bytes 3145736 | tf_op jit(solution)/shard_map/while/body/eval_jaxpr/ppermute | solution.py:10
  286.8 13.2 %copy-start.1 = (bf16[1024,1024]{1,0:T(8,128)(2,1)S(1)}, bf16[1024,1024]{1,0:T(8,128)(2,1)}, u32[]{:S(2)}) copy-start(bf16[1024,1024]{1,0:T(8,128)(2,1)} %get-tuple-element.365) | copy-start | bytes 6291460 | tf_op jit(solution)/shard_map/while
  306.2 17.2 %collective-permute-start = (bf16[1024,2,256]{2,0,1:T(8,128)(2,1)}, bf16[1024,2,256]{2,0,1:T(8,128)(2,1)S(1)}, u32[]{:S(2)}, u32[]{:S(2)}) collective-permute-start(bf16[1024,2,256]{2,0,1:T(8,128)(2,1)} %copy.45), channel_id=1, source_target_pairs={{0,4},{4,8},{8,12},{12,16},{16,20},{20,24},{24,28},{1,5},{5,9},{9,... | collective-permute-start | bytes 3145736 | tf_op jit(solution)/shard_map/while/body/eval_jaxpr/ppermute | solution.py:10
  312.2 13.2 %copy-start.1 = (bf16[1024,1024]{1,0:T(8,128)(2,1)S(1)}, bf16[1024,1024]{1,0:T(8,128)(2,1)}, u32[]{:S(2)}) copy-start(bf16[1024,1024]{1,0:T(8,128)(2,1)} %get-tuple-element.365) | copy-start | bytes 6291460 | tf_op jit(solution)/shard_map/while
  331.7 17.6 %collective-permute-start = (bf16[1024,2,256]{2,0,1:T(8,128)(2,1)}, bf16[1024,2,256]{2,0,1:T(8,128)(2,1)S(1)}, u32[]{:S(2)}, u32[]{:S(2)}) collective-permute-start(bf16[1024,2,256]{2,0,1:T(8,128)(2,1)} %copy.45), channel_id=1, source_target_pairs={{0,4},{4,8},{8,12},{12,16},{16,20},{20,24},{24,28},{1,5},{5,9},{9,... | collective-permute-start | bytes 3145736 | tf_op jit(solution)/shard_map/while/body/eval_jaxpr/ppermute | solution.py:10
  337.7 13.5 %copy-start.1 = (bf16[1024,1024]{1,0:T(8,128)(2,1)S(1)}, bf16[1024,1024]{1,0:T(8,128)(2,1)}, u32[]{:S(2)}) copy-start(bf16[1024,1024]{1,0:T(8,128)(2,1)} %get-tuple-element.365) | copy-start | bytes 6291460 | tf_op jit(solution)/shard_map/while
  361.1 17.2 %collective-permute-start = (bf16[1024,2,256]{2,0,1:T(8,128)(2,1)}, bf16[1024,2,256]{2,0,1:T(8,128)(2,1)S(1)}, u32[]{:S(2)}, u32[]{:S(2)}) collective-permute-start(bf16[1024,2,256]{2,0,1:T(8,128)(2,1)} %copy.45), channel_id=1, source_target_pairs={{0,4},{4,8},{8,12},{12,16},{16,20},{20,24},{24,28},{1,5},{5,9},{9,... | collective-permute-start | bytes 3145736 | tf_op jit(solution)/shard_map/while/body/eval_jaxpr/ppermute | solution.py:10
  367.1 13.2 %copy-start.1 = (bf16[1024,1024]{1,0:T(8,128)(2,1)S(1)}, bf16[1024,1024]{1,0:T(8,128)(2,1)}, u32[]{:S(2)}) copy-start(bf16[1024,1024]{1,0:T(8,128)(2,1)} %get-tuple-element.365) | copy-start | bytes 6291460 | tf_op jit(solution)/shard_map/while
  390.2 17.2 %collective-permute-start = (bf16[1024,2,256]{2,0,1:T(8,128)(2,1)}, bf16[1024,2,256]{2,0,1:T(8,128)(2,1)S(1)}, u32[]{:S(2)}, u32[]{:S(2)}) collective-permute-start(bf16[1024,2,256]{2,0,1:T(8,128)(2,1)} %copy.45), channel_id=1, source_target_pairs={{0,4},{4,8},{8,12},{12,16},{16,20},{20,24},{24,28},{1,5},{5,9},{9,... | collective-permute-start | bytes 3145736 | tf_op jit(solution)/shard_map/while/body/eval_jaxpr/ppermute | solution.py:10
  396.2 13.2 %copy-start.1 = (bf16[1024,1024]{1,0:T(8,128)(2,1)S(1)}, bf16[1024,1024]{1,0:T(8,128)(2,1)}, u32[]{:S(2)}) copy-start(bf16[1024,1024]{1,0:T(8,128)(2,1)} %get-tuple-element.365) | copy-start | bytes 6291460 | tf_op jit(solution)/shard_map/while
  419.3 17.2 %collective-permute-start = (bf16[1024,2,256]{2,0,1:T(8,128)(2,1)}, bf16[1024,2,256]{2,0,1:T(8,128)(2,1)S(1)}, u32[]{:S(2)}, u32[]{:S(2)}) collective-permute-start(bf16[1024,2,256]{2,0,1:T(8,128)(2,1)} %copy.45), channel_id=1, source_target_pairs={{0,4},{4,8},{8,12},{12,16},{16,20},{20,24},{24,28},{1,5},{5,9},{9,... | collective-permute-start | bytes 3145736 | tf_op jit(solution)/shard_map/while/body/eval_jaxpr/ppermute | solution.py:10
  425.3 13.2 %copy-start.1 = (bf16[1024,1024]{1,0:T(8,128)(2,1)S(1)}, bf16[1024,1024]{1,0:T(8,128)(2,1)}, u32[]{:S(2)}) copy-start(bf16[1024,1024]{1,0:T(8,128)(2,1)} %get-tuple-element.365) | copy-start | bytes 6291460 | tf_op jit(solution)/shard_map/while
  448.3 17.2 %collective-permute-start = (bf16[1024,2,256]{2,0,1:T(8,128)(2,1)}, bf16[1024,2,256]{2,0,1:T(8,128)(2,1)S(1)}, u32[]{:S(2)}, u32[]{:S(2)}) collective-permute-start(bf16[1024,2,256]{2,0,1:T(8,128)(2,1)} %copy.45), channel_id=1, source_target_pairs={{0,4},{4,8},{8,12},{12,16},{16,20},{20,24},{24,28},{1,5},{5,9},{9,... | collective-permute-start | bytes 3145736 | tf_op jit(solution)/shard_map/while/body/eval_jaxpr/ppermute | solution.py:10
  454.4 13.2 %copy-start.1 = (bf16[1024,1024]{1,0:T(8,128)(2,1)S(1)}, bf16[1024,1024]{1,0:T(8,128)(2,1)}, u32[]{:S(2)}) copy-start(bf16[1024,1024]{1,0:T(8,128)(2,1)} %get-tuple-element.365) | copy-start | bytes 6291460 | tf_op jit(solution)/shard_map/while
  477.4 17.2 %collective-permute-start = (bf16[1024,2,256]{2,0,1:T(8,128)(2,1)}, bf16[1024,2,256]{2,0,1:T(8,128)(2,1)S(1)}, u32[]{:S(2)}, u32[]{:S(2)}) collective-permute-start(bf16[1024,2,256]{2,0,1:T(8,128)(2,1)} %copy.45), channel_id=1, source_target_pairs={{0,4},{4,8},{8,12},{12,16},{16,20},{20,24},{24,28},{1,5},{5,9},{9,... | collective-permute-start | bytes 3145736 | tf_op jit(solution)/shard_map/while/body/eval_jaxpr/ppermute | solution.py:10
  483.4 13.2 %copy-start.1 = (bf16[1024,1024]{1,0:T(8,128)(2,1)S(1)}, bf16[1024,1024]{1,0:T(8,128)(2,1)}, u32[]{:S(2)}) copy-start(bf16[1024,1024]{1,0:T(8,128)(2,1)} %get-tuple-element.365) | copy-start | bytes 6291460 | tf_op jit(solution)/shard_map/while
  506.5 17.2 %collective-permute-start = (bf16[1024,2,256]{2,0,1:T(8,128)(2,1)}, bf16[1024,2,256]{2,0,1:T(8,128)(2,1)S(1)}, u32[]{:S(2)}, u32[]{:S(2)}) collective-permute-start(bf16[1024,2,256]{2,0,1:T(8,128)(2,1)} %copy.45), channel_id=1, source_target_pairs={{0,4},{4,8},{8,12},{12,16},{16,20},{20,24},{24,28},{1,5},{5,9},{9,... | collective-permute-start | bytes 3145736 | tf_op jit(solution)/shard_map/while/body/eval_jaxpr/ppermute | solution.py:10
  512.5 13.2 %copy-start.1 = (bf16[1024,1024]{1,0:T(8,128)(2,1)S(1)}, bf16[1024,1024]{1,0:T(8,128)(2,1)}, u32[]{:S(2)}) copy-start(bf16[1024,1024]{1,0:T(8,128)(2,1)} %get-tuple-element.365) | copy-start | bytes 6291460 | tf_op jit(solution)/shard_map/while
  532.0 17.2 %collective-permute-start = (bf16[1024,2,256]{2,0,1:T(8,128)(2,1)}, bf16[1024,2,256]{2,0,1:T(8,128)(2,1)S(1)}, u32[]{:S(2)}, u32[]{:S(2)}) collective-permute-start(bf16[1024,2,256]{2,0,1:T(8,128)(2,1)} %copy.45), channel_id=1, source_target_pairs={{0,4},{4,8},{8,12},{12,16},{16,20},{20,24},{24,28},{1,5},{5,9},{9,... | collective-permute-start | bytes 3145736 | tf_op jit(solution)/shard_map/while/body/eval_jaxpr/ppermute | solution.py:10
  538.0 13.2 %copy-start.1 = (bf16[1024,1024]{1,0:T(8,128)(2,1)S(1)}, bf16[1024,1024]{1,0:T(8,128)(2,1)}, u32[]{:S(2)}) copy-start(bf16[1024,1024]{1,0:T(8,128)(2,1)} %get-tuple-element.365) | copy-start | bytes 6291460 | tf_op jit(solution)/shard_map/while
  557.4 17.2 %collective-permute-start = (bf16[1024,2,256]{2,0,1:T(8,128)(2,1)}, bf16[1024,2,256]{2,0,1:T(8,128)(2,1)S(1)}, u32[]{:S(2)}, u32[]{:S(2)}) collective-permute-start(bf16[1024,2,256]{2,0,1:T(8,128)(2,1)} %copy.45), channel_id=1, source_target_pairs={{0,4},{4,8},{8,12},{12,16},{16,20},{20,24},{24,28},{1,5},{5,9},{9,... | collective-permute-start | bytes 3145736 | tf_op jit(solution)/shard_map/while/body/eval_jaxpr/ppermute | solution.py:10
  563.4 13.2 %copy-start.1 = (bf16[1024,1024]{1,0:T(8,128)(2,1)S(1)}, bf16[1024,1024]{1,0:T(8,128)(2,1)}, u32[]{:S(2)}) copy-start(bf16[1024,1024]{1,0:T(8,128)(2,1)} %get-tuple-element.365) | copy-start | bytes 6291460 | tf_op jit(solution)/shard_map/while
Sparse Core Ops, SparseCore 0:
  35.6 86.7 all-gather.1
where the time goes:
time: 746 us; the launch traced here: 744 us
  blocking collectives  275 us (37%)
  local copies, waits for them, and re-layouts  206 us (28%)
  waiting for transfers between devices  166 us (22%)
  other arithmetic  38.1 us (5%)
  starting transfers between devices  30.2 us (4%)
  matrix products  13.9 us (2%)
  between operations  13.4 us (2%)
    all_gather x1, blocking collectives, per_device(): lax.all_gather(thresholds, 'ch', axis=1, tiled=True)  140 us
    ppermute x13, waiting for transfers between devices, passed_along(): lax.ppermute(value, axis, [(source, source + steps) for source in range(l...  134 us
    all_to_all x1, blocking collectives, per_device(): lax.all_to_all(final_pair[1], 'ch', split_axis=1, concat_axis=3, tiled=True)  134 us
    dynamic_slice x26, local copies, waits for them, and re-layouts, step(): previous = lax.dynamic_index_in_dim(stored, energy_slot, 0, keepdims=False)  44.3 us
    dynamic_update_slice x26, local copies, waits for them, and re-layouts, step(): stored = lax.dynamic_update_index_in_dim(stored, kept, energy_slot, 0)  34.2 us
    all_to_all x1, waiting for transfers between devices, per_device(): lax.all_to_all(paired, 'ch', split_axis=3, concat_axis=1, tiled=True)  31.1 us
    another operation x13, local copies, waits for them, and re-layouts  29.2 us
    ppermute x13, starting transfers between devices, passed_along(): lax.ppermute(value, axis, [(source, source + steps) for source in range(l...  24.8 us
  transfers between devices with their start and end apart: 15, of which 14 were waited for; matrix products, arithmetic and copies ran while one was open for 11% of the time, Pallas kernels for 0%

commit v1 on v0

--- a/solution.py
+++ b/solution.py
@@ -28,7 +28,9 @@
     channel_thresholds = thresholds_whole[0].astype(jnp.float32)
     channel_count = basis_change.shape[0]
     paired = start_amps.reshape(energy_count, row_count, 2, half_cols)
-    start_cols = lax.all_to_all(paired, "ch", split_axis=3, concat_axis=1, tiled=True)
+    parts = jnp.split(paired, lax.axis_size("ch"), axis=3)
+    received = lax.all_to_all(jnp.stack(parts), "ch", 0, 0)
+    start_cols = jnp.concatenate(received, axis=1)
     stored_init = jnp.zeros((energy_count, channel_count, 2, col_width), jnp.bfloat16)
 
     def multiply(flat):

time: 746 us -> 746 us (level)
  local copies, waits for them, and re-layouts: 206 us -> 192 us
  other arithmetic: 38.1 us -> 48.7 us
    another operation x0 -> x1, other arithmetic: none -> 12.5 us  [per_device(): received = lax.all_to_all(jnp.stack(parts), 'ch', 0, 0)]
    unnamed x5 -> x4, local copies, waits for them, and re-layouts: 8.61 us -> 0.01 us
    all_to_all x2 -> x1, local copies, waits for them, and re-layouts: 15 us -> 6.63 us  [per_device(): received = lax.all_to_all(jnp.stack(parts), 'ch', 0, 0)]
    another operation x13 -> x14, local copies, waits for them, and re-layouts: 29.2 us -> 35.3 us
  transfers between devices with their start and end apart: 15 -> 15, of which waited for: 14 -> 14; matrix products, arithmetic and copies ran while one was open for 11% -> 9% of each run, Pallas kernels for 0% -> 0%
where the time goes in v1:
time: 746 us; the launch traced here: 744 us
  blocking collectives  275 us (37%)
  local copies, waits for them, and re-layouts  192 us (26%)
  waiting for transfers between devices  169 us (23%)
  other arithmetic  48.7 us (7%)
  starting transfers between devices  30.2 us (4%)
  matrix products  13.9 us (2%)
  between operations  13.4 us (2%)
    all_gather x1, blocking collectives, per_device(): lax.all_gather(thresholds, 'ch', axis=1, tiled=True)  140 us
    ppermute x13, waiting for transfers between devices, passed_along(): lax.ppermute(value, axis, [(source, source + steps) for source in range(l...  138 us
    all_to_all x1, blocking collectives, per_device(): lax.all_to_all(final_pair[1], 'ch', split_axis=1, concat_axis=3, tiled=True)  134 us
    dynamic_slice x26, local copies, waits for them, and re-layouts, step(): previous = lax.dynamic_index_in_dim(stored, energy_slot, 0, keepdims=False)  44.3 us
    dynamic_update_slice x26, local copies, waits for them, and re-layouts, step(): stored = lax.dynamic_update_index_in_dim(stored, kept, energy_slot, 0)  34.2 us
    all_to_all x1, waiting for transfers between devices, per_device(): received = lax.all_to_all(jnp.stack(parts), 'ch', 0, 0)  31.1 us
    another operation x13, local copies, waits for them, and re-layouts  29.4 us
    ppermute x13, starting transfers between devices, passed_along(): lax.ppermute(value, axis, [(source, source + steps) for source in range(l...  24.8 us
  transfers between devices with their start and end apart: 15, of which 14 were waited for; matrix products, arithmetic and copies ran while one was open for 9% of the time, Pallas kernels for 0%

profile of v1, /device:TPU:4, one launch (start us, length us, event | category | flops | bytes accessed | tf_op | source)
XLA Modules:
  0.0 743.5 jit_solution(12281299105284059435)
XLA Ops:
  6.5 11.1 %reshape.111 = bf16[6,256,2,1024]{3,2,1,0:T(2,128)(2,1)} reshape(bf16[6,256,2048]{2,1,0:T(8,128)(2,1)} %param.8) | data formatting | bytes 12582912 | tf_op jit(solution)/shard_map/reshape | solution.py:30
  17.6 5.9 slice_bitcast_fusion.3
  23.6 12.5 %pad_maximum_fusion.1 = bf16[4,6,256,2,256]{4,3,2,1,0:T(2,128)(2,1)} fusion(bf16[1,6,256,2,256]{4,3,2,1,0:T(2,128)(2,1)S(1)} %get-tuple-element.241, bf16[1,6,256,2,256]{4,3,2,1,0:T(2,128)(2,1)S(1)} %get-tuple-element.242, bf16[1,6,256,2,256]{4,3,2,1,0:T(2,128)(2,1)S(1)} %get-tuple-element.243, bf16[1,6,256,2,256]{4,3,2,1,0:T(2,128)(2,1)S(1)} %get-tuple-element.240), kind=kLoop, calls=%fused_computation.14 | loop fusion | flops 9437184 | bytes 12582912 | tf_op jit(solution)/shard_map/stack | solution.py:32
  36.1 5.4 all-to-all-start
  42.2 140.4 %all_gather.6 = bf16[1,1024]{1,0:T(2,128)(2,1)S(1)} all-gather(bf16[1,256]{1,0:T(2,128)(2,1)S(1)} %copy-done), channel_id=1, replica_groups=mesh['sec'=8,'ch'=4] {'ch'}, dimensions={1}, use_global_device_ids=true | all-gather | bytes 2560 | tf_op jit(solution)/shard_map/all_gather | solution.py:25
  182.6 31.1 %all-to-all-done = bf16[4,6,256,2,256]{4,3,2,1,0:T(2,128)(2,1)} async-done(((bf16[4,6,256,2,256]{4,3,2,1,0:T(2,128)(2,1)}), bf16[4,6,256,2,256]{4,3,2,1,0:T(2,128)(2,1)}, u32[]{:S(2)}, u32[]{:S(2)}) %all-to-all-start) | async-done | bytes 6291488 | tf_op jit(solution)/shard_map/all_to_all | solution.py:32
  213.6 6.6 copy.20
  221.4 5.9 broadcast_in_dim.14.clone
  227.3 353.3 %while.16 = (s32[]{:T(128)}, bf16[1024,2,256]{0,2,1:T(8,128)(2,1)}, bf16[6,1024,2,256]{3,2,0,1:T(2,128)(2,1)}, s32[]{:T(128)}, f32[6]{0:T(128)S(1)}, /*index=5*/...) while((s32[]{:T(128)}, bf16[1024,2,256]{0,2,1:T(8,128)(2,1)}, ...), condition=%wide.region_3.4_spmd, body=%wide.region_0.3_spmd.sunk | while | flops 1078464512 | bytes 46166332 | solution.py:67
  227.3 2.3 copy.31
  236.3 10.6 %collective-permute-done = bf16[1024,2,256]{2,0,1:T(8,128)(2,1)S(1)} collective-permute-done((bf16[1024,2,256]{2,0,1:T(8,128)(2,1)}, bf16[1024,2,256]{2,0,1:T(8,128)(2,1)S(1)}, u32[]{:S(2)}, u32[]{:S(2)}) %collective-permute-start) | collective-permute-done | bytes 1048608 | tf_op jit(solution)/shard_map/while/body/eval_jaxpr/ppermute | solution.py:10
  252.8 2.3 copy.31
  261.7 10.6 %collective-permute-done = bf16[1024,2,256]{2,0,1:T(8,128)(2,1)S(1)} collective-permute-done((bf16[1024,2,256]{2,0,1:T(8,128)(2,1)}, bf16[1024,2,256]{2,0,1:T(8,128)(2,1)S(1)}, u32[]{:S(2)}, u32[]{:S(2)}) %collective-permute-start) | collective-permute-done | bytes 1048608 | tf_op jit(solution)/shard_map/while/body/eval_jaxpr/ppermute | solution.py:10
  278.3 2.3 copy.31
  287.2 10.6 %collective-permute-done = bf16[1024,2,256]{2,0,1:T(8,128)(2,1)S(1)} collective-permute-done((bf16[1024,2,256]{2,0,1:T(8,128)(2,1)}, bf16[1024,2,256]{2,0,1:T(8,128)(2,1)S(1)}, u32[]{:S(2)}, u32[]{:S(2)}) %collective-permute-start) | collective-permute-done | bytes 1048608 | tf_op jit(solution)/shard_map/while/body/eval_jaxpr/ppermute | solution.py:10
  303.8 2.3 copy.31
  312.7 10.6 %collective-permute-done = bf16[1024,2,256]{2,0,1:T(8,128)(2,1)S(1)} collective-permute-done((bf16[1024,2,256]{2,0,1:T(8,128)(2,1)}, bf16[1024,2,256]{2,0,1:T(8,128)(2,1)S(1)}, u32[]{:S(2)}, u32[]{:S(2)}) %collective-permute-start) | collective-permute-done | bytes 1048608 | tf_op jit(solution)/shard_map/while/body/eval_jaxpr/ppermute | solution.py:10
  329.3 2.3 copy.31
  338.2 10.9 %collective-permute-done = bf16[1024,2,256]{2,0,1:T(8,128)(2,1)S(1)} collective-permute-done((bf16[1024,2,256]{2,0,1:T(8,128)(2,1)}, bf16[1024,2,256]{2,0,1:T(8,128)(2,1)S(1)}, u32[]{:S(2)}, u32[]{:S(2)}) %collective-permute-start) | collective-permute-done | bytes 1048608 | tf_op jit(solution)/shard_map/while/body/eval_jaxpr/ppermute | solution.py:10
  351.1 4.9 conditional.2
  352.4 2.3 convolution_convert_fusion
  358.7 2.3 copy.31
  367.6 10.6 %collective-permute-done = bf16[1024,2,256]{2,0,1:T(8,128)(2,1)S(1)} collective-permute-done((bf16[1024,2,256]{2,0,1:T(8,128)(2,1)}, bf16[1024,2,256]{2,0,1:T(8,128)(2,1)S(1)}, u32[]{:S(2)}, u32[]{:S(2)}) %collective-permute-start) | collective-permute-done | bytes 1048608 | tf_op jit(solution)/shard_map/while/body/eval_jaxpr/ppermute | solution.py:10
  380.1 4.9 conditional.2
  381.5 2.3 convolution_convert_fusion
  387.8 2.3 copy.31
  396.7 10.6 %collective-permute-done = bf16[1024,2,256]{2,0,1:T(8,128)(2,1)S(1)} collective-permute-done((bf16[1024,2,256]{2,0,1:T(8,128)(2,1)}, bf16[1024,2,256]{2,0,1:T(8,128)(2,1)S(1)}, u32[]{:S(2)}, u32[]{:S(2)}) %collective-permute-start) | collective-permute-done | bytes 1048608 | tf_op jit(solution)/shard_map/while/body/eval_jaxpr/ppermute | solution.py:10
  409.2 4.9 conditional.2
  410.6 2.3 convolution_convert_fusion
  416.9 2.3 copy.31
  425.8 10.6 %collective-permute-done = bf16[1024,2,256]{2,0,1:T(8,128)(2,1)S(1)} collective-permute-done((bf16[1024,2,256]{2,0,1:T(8,128)(2,1)}, bf16[1024,2,256]{2,0,1:T(8,128)(2,1)S(1)}, u32[]{:S(2)}, u32[]{:S(2)}) %collective-permute-start) | collective-permute-done | bytes 1048608 | tf_op jit(solution)/shard_map/while/body/eval_jaxpr/ppermute | solution.py:10
  438.3 4.9 conditional.2
  439.7 2.3 convolution_convert_fusion
  454.9 10.6 %collective-permute-done = bf16[1024,2,256]{2,0,1:T(8,128)(2,1)S(1)} collective-permute-done((bf16[1024,2,256]{2,0,1:T(8,128)(2,1)}, bf16[1024,2,256]{2,0,1:T(8,128)(2,1)S(1)}, u32[]{:S(2)}, u32[]{:S(2)}) %collective-permute-start) | collective-permute-done | bytes 1048608 | tf_op jit(solution)/shard_map/while/body/eval_jaxpr/ppermute | solution.py:10
  467.4 4.9 conditional.2
  468.8 2.3 convolution_convert_fusion
  484.0 10.6 %collective-permute-done = bf16[1024,2,256]{2,0,1:T(8,128)(2,1)S(1)} collective-permute-done((bf16[1024,2,256]{2,0,1:T(8,128)(2,1)}, bf16[1024,2,256]{2,0,1:T(8,128)(2,1)S(1)}, u32[]{:S(2)}, u32[]{:S(2)}) %collective-permute-start) | collective-permute-done | bytes 1048608 | tf_op jit(solution)/shard_map/while/body/eval_jaxpr/ppermute | solution.py:10
  496.5 4.9 conditional.2
  497.9 2.3 convolution_convert_fusion
  504.2 2.3 copy.31
  513.1 10.6 %collective-permute-done = bf16[1024,2,256]{2,0,1:T(8,128)(2,1)S(1)} collective-permute-done((bf16[1024,2,256]{2,0,1:T(8,128)(2,1)}, bf16[1024,2,256]{2,0,1:T(8,128)(2,1)S(1)}, u32[]{:S(2)}, u32[]{:S(2)}) %collective-permute-start) | collective-permute-done | bytes 1048608 | tf_op jit(solution)/shard_map/while/body/eval_jaxpr/ppermute | solution.py:10
  529.7 2.3 copy.31
  538.6 10.6 %collective-permute-done = bf16[1024,2,256]{2,0,1:T(8,128)(2,1)S(1)} collective-permute-done((bf16[1024,2,256]{2,0,1:T(8,128)(2,1)}, bf16[1024,2,256]{2,0,1:T(8,128)(2,1)S(1)}, u32[]{:S(2)}, u32[]{:S(2)}) %collective-permute-start) | collective-permute-done | bytes 1048608 | tf_op jit(solution)/shard_map/while/body/eval_jaxpr/ppermute | solution.py:10
  555.1 2.3 copy.31
  564.1 10.6 %collective-permute-done = bf16[1024,2,256]{2,0,1:T(8,128)(2,1)S(1)} collective-permute-done((bf16[1024,2,256]{2,0,1:T(8,128)(2,1)}, bf16[1024,2,256]{2,0,1:T(8,128)(2,1)S(1)}, u32[]{:S(2)}, u32[]{:S(2)}) %collective-permute-start) | collective-permute-done | bytes 1048608 | tf_op jit(solution)/shard_map/while/body/eval_jaxpr/ppermute | solution.py:10
  580.6 134.3 %all_to_all.20 = bf16[6,1024,2,256]{3,2,0,1:T(2,128)(2,1)S(1)} all-to-all(bf16[6,1024,2,256]{3,2,0,1:T(2,128)(2,1)} %get-tuple-element.205), channel_id=1, replica_groups=mesh['sec'=8,'ch'=4] {'ch'}, dimensions={1} | all-to-all | bytes 12582912 | tf_op jit(solution)/shard_map/all_to_all | solution.py:68
  714.9 10.7 %copy.22 = bf16[6,256,2,4,256]{4,3,2,1,0:T(4,128)(2,1)} copy(bf16[6,256,2,4,256]{4,2,0,1,3:T(2,128)(2,1)S(1)} %bitcast.33) | data formatting | bytes 12582912 | tf_op jit(solution)/shard_map/all_to_all | solution.py:68
  725.7 11.0 %broadcast_in_dim_reshape.3 = bf16[1,6,256,2048]{3,2,1,0:T(8,128)(2,1)} reshape(bf16[6,256,2,4,256]{4,3,2,1,0:T(4,128)(2,1)} %copy.22) | data formatting | bytes 12582912 | tf_op jit(solution)/shard_map/broadcast_in_dim;reshape | solution.py:69
  (219 shorter events, 186.4 us)
Async XLA Ops:
  36.1 6.1 copy-start
  36.1 177.6 %all-to-all-start = ((bf16[4,6,256,2,256]{4,3,2,1,0:T(2,128)(2,1)}), bf16[4,6,256,2,256]{4,3,2,1,0:T(2,128)(2,1)}, u32[]{:S(2)}, u32[]{:S(2)}) async-start(bf16[4,6,256,2,256]{4,3,2,1,0:T(2,128)(2,1)} %pad_maximum_fusion.1), calls=%async_computation | async-start | bytes 12582912 | tf_op jit(solution)/shard_map/all_to_all | solution.py:32
  41.4 178.8 %all-gather.2.cloned.1.call-start = ((), (), s32[]{:S(2)}) async-start(), calls=%async_computation.2 | async-start | bytes 2621440 | tf_op jit(solution)/shard_map/all_gather | solution.py:24
  220.2 7.1 copy-start.2
  229.6 17.2 %collective-permute-start = (bf16[1024,2,256]{2,0,1:T(8,128)(2,1)}, bf16[1024,2,256]{2,0,1:T(8,128)(2,1)S(1)}, u32[]{:S(2)}, u32[]{:S(2)}) collective-permute-start(bf16[1024,2,256]{2,0,1:T(8,128)(2,1)} %copy.31), channel_id=1, source_target_pairs={{0,4},{4,8},{8,12},{12,16},{16,20},{20,24},{24,28},{1,5},{5,9},{9,... | collective-permute-start | bytes 3145736 | tf_op jit(solution)/shard_map/while/body/eval_jaxpr/ppermute | solution.py:10
  235.5 13.3 %copy-start.1 = (bf16[1024,1024]{1,0:T(8,128)(2,1)S(1)}, bf16[1024,1024]{1,0:T(8,128)(2,1)}, u32[]{:S(2)}) copy-start(bf16[1024,1024]{1,0:T(8,128)(2,1)} %get-tuple-element.351) | copy-start | bytes 6291460 | tf_op jit(solution)/shard_map/while
  255.1 17.2 %collective-permute-start = (bf16[1024,2,256]{2,0,1:T(8,128)(2,1)}, bf16[1024,2,256]{2,0,1:T(8,128)(2,1)S(1)}, u32[]{:S(2)}, u32[]{:S(2)}) collective-permute-start(bf16[1024,2,256]{2,0,1:T(8,128)(2,1)} %copy.31), channel_id=1, source_target_pairs={{0,4},{4,8},{8,12},{12,16},{16,20},{20,24},{24,28},{1,5},{5,9},{9,... | collective-permute-start | bytes 3145736 | tf_op jit(solution)/shard_map/while/body/eval_jaxpr/ppermute | solution.py:10
  261.0 13.3 %copy-start.1 = (bf16[1024,1024]{1,0:T(8,128)(2,1)S(1)}, bf16[1024,1024]{1,0:T(8,128)(2,1)}, u32[]{:S(2)}) copy-start(bf16[1024,1024]{1,0:T(8,128)(2,1)} %get-tuple-element.351) | copy-start | bytes 6291460 | tf_op jit(solution)/shard_map/while
  280.6 17.2 %collective-permute-start = (bf16[1024,2,256]{2,0,1:T(8,128)(2,1)}, bf16[1024,2,256]{2,0,1:T(8,128)(2,1)S(1)}, u32[]{:S(2)}, u32[]{:S(2)}) collective-permute-start(bf16[1024,2,256]{2,0,1:T(8,128)(2,1)} %copy.31), channel_id=1, source_target_pairs={{0,4},{4,8},{8,12},{12,16},{16,20},{20,24},{24,28},{1,5},{5,9},{9,... | collective-permute-start | bytes 3145736 | tf_op jit(solution)/shard_map/while/body/eval_jaxpr/ppermute | solution.py:10
  286.5 13.3 %copy-start.1 = (bf16[1024,1024]{1,0:T(8,128)(2,1)S(1)}, bf16[1024,1024]{1,0:T(8,128)(2,1)}, u32[]{:S(2)}) copy-start(bf16[1024,1024]{1,0:T(8,128)(2,1)} %get-tuple-element.351) | copy-start | bytes 6291460 | tf_op jit(solution)/shard_map/while
  306.0 17.2 %collective-permute-start = (bf16[1024,2,256]{2,0,1:T(8,128)(2,1)}, bf16[1024,2,256]{2,0,1:T(8,128)(2,1)S(1)}, u32[]{:S(2)}, u32[]{:S(2)}) collective-permute-start(bf16[1024,2,256]{2,0,1:T(8,128)(2,1)} %copy.31), channel_id=1, source_target_pairs={{0,4},{4,8},{8,12},{12,16},{16,20},{20,24},{24,28},{1,5},{5,9},{9,... | collective-permute-start | bytes 3145736 | tf_op jit(solution)/shard_map/while/body/eval_jaxpr/ppermute | solution.py:10
  311.9 13.3 %copy-start.1 = (bf16[1024,1024]{1,0:T(8,128)(2,1)S(1)}, bf16[1024,1024]{1,0:T(8,128)(2,1)}, u32[]{:S(2)}) copy-start(bf16[1024,1024]{1,0:T(8,128)(2,1)} %get-tuple-element.351) | copy-start | bytes 6291460 | tf_op jit(solution)/shard_map/while
  331.5 17.6 %collective-permute-start = (bf16[1024,2,256]{2,0,1:T(8,128)(2,1)}, bf16[1024,2,256]{2,0,1:T(8,128)(2,1)S(1)}, u32[]{:S(2)}, u32[]{:S(2)}) collective-permute-start(bf16[1024,2,256]{2,0,1:T(8,128)(2,1)} %copy.31), channel_id=1, source_target_pairs={{0,4},{4,8},{8,12},{12,16},{16,20},{20,24},{24,28},{1,5},{5,9},{9,... | collective-permute-start | bytes 3145736 | tf_op jit(solution)/shard_map/while/body/eval_jaxpr/ppermute | solution.py:10
  337.4 13.6 %copy-start.1 = (bf16[1024,1024]{1,0:T(8,128)(2,1)S(1)}, bf16[1024,1024]{1,0:T(8,128)(2,1)}, u32[]{:S(2)}) copy-start(bf16[1024,1024]{1,0:T(8,128)(2,1)} %get-tuple-element.351) | copy-start | bytes 6291460 | tf_op jit(solution)/shard_map/while
  361.0 17.2 %collective-permute-start = (bf16[1024,2,256]{2,0,1:T(8,128)(2,1)}, bf16[1024,2,256]{2,0,1:T(8,128)(2,1)S(1)}, u32[]{:S(2)}, u32[]{:S(2)}) collective-permute-start(bf16[1024,2,256]{2,0,1:T(8,128)(2,1)} %copy.31), channel_id=1, source_target_pairs={{0,4},{4,8},{8,12},{12,16},{16,20},{20,24},{24,28},{1,5},{5,9},{9,... | collective-permute-start | bytes 3145736 | tf_op jit(solution)/shard_map/while/body/eval_jaxpr/ppermute | solution.py:10
  366.9 13.3 %copy-start.1 = (bf16[1024,1024]{1,0:T(8,128)(2,1)S(1)}, bf16[1024,1024]{1,0:T(8,128)(2,1)}, u32[]{:S(2)}) copy-start(bf16[1024,1024]{1,0:T(8,128)(2,1)} %get-tuple-element.351) | copy-start | bytes 6291460 | tf_op jit(solution)/shard_map/while
  390.1 17.2 %collective-permute-start = (bf16[1024,2,256]{2,0,1:T(8,128)(2,1)}, bf16[1024,2,256]{2,0,1:T(8,128)(2,1)S(1)}, u32[]{:S(2)}, u32[]{:S(2)}) collective-permute-start(bf16[1024,2,256]{2,0,1:T(8,128)(2,1)} %copy.31), channel_id=1, source_target_pairs={{0,4},{4,8},{8,12},{12,16},{16,20},{20,24},{24,28},{1,5},{5,9},{9,... | collective-permute-start | bytes 3145736 | tf_op jit(solution)/shard_map/while/body/eval_jaxpr/ppermute | solution.py:10
  396.0 13.3 %copy-start.1 = (bf16[1024,1024]{1,0:T(8,128)(2,1)S(1)}, bf16[1024,1024]{1,0:T(8,128)(2,1)}, u32[]{:S(2)}) copy-start(bf16[1024,1024]{1,0:T(8,128)(2,1)} %get-tuple-element.351) | copy-start | bytes 6291460 | tf_op jit(solution)/shard_map/while
  419.2 17.2 %collective-permute-start = (bf16[1024,2,256]{2,0,1:T(8,128)(2,1)}, bf16[1024,2,256]{2,0,1:T(8,128)(2,1)S(1)}, u32[]{:S(2)}, u32[]{:S(2)}) collective-permute-start(bf16[1024,2,256]{2,0,1:T(8,128)(2,1)} %copy.31), channel_id=1, source_target_pairs={{0,4},{4,8},{8,12},{12,16},{16,20},{20,24},{24,28},{1,5},{5,9},{9,... | collective-permute-start | bytes 3145736 | tf_op jit(solution)/shard_map/while/body/eval_jaxpr/ppermute | solution.py:10
  425.1 13.3 %copy-start.1 = (bf16[1024,1024]{1,0:T(8,128)(2,1)S(1)}, bf16[1024,1024]{1,0:T(8,128)(2,1)}, u32[]{:S(2)}) copy-start(bf16[1024,1024]{1,0:T(8,128)(2,1)} %get-tuple-element.351) | copy-start | bytes 6291460 | tf_op jit(solution)/shard_map/while
  448.3 17.2 %collective-permute-start = (bf16[1024,2,256]{2,0,1:T(8,128)(2,1)}, bf16[1024,2,256]{2,0,1:T(8,128)(2,1)S(1)}, u32[]{:S(2)}, u32[]{:S(2)}) collective-permute-start(bf16[1024,2,256]{2,0,1:T(8,128)(2,1)} %copy.31), channel_id=1, source_target_pairs={{0,4},{4,8},{8,12},{12,16},{16,20},{20,24},{24,28},{1,5},{5,9},{9,... | collective-permute-start | bytes 3145736 | tf_op jit(solution)/shard_map/while/body/eval_jaxpr/ppermute | solution.py:10
  454.2 13.3 %copy-start.1 = (bf16[1024,1024]{1,0:T(8,128)(2,1)S(1)}, bf16[1024,1024]{1,0:T(8,128)(2,1)}, u32[]{:S(2)}) copy-start(bf16[1024,1024]{1,0:T(8,128)(2,1)} %get-tuple-element.351) | copy-start | bytes 6291460 | tf_op jit(solution)/shard_map/while
  477.3 17.2 %collective-permute-start = (bf16[1024,2,256]{2,0,1:T(8,128)(2,1)}, bf16[1024,2,256]{2,0,1:T(8,128)(2,1)S(1)}, u32[]{:S(2)}, u32[]{:S(2)}) collective-permute-start(bf16[1024,2,256]{2,0,1:T(8,128)(2,1)} %copy.31), channel_id=1, source_target_pairs={{0,4},{4,8},{8,12},{12,16},{16,20},{20,24},{24,28},{1,5},{5,9},{9,... | collective-permute-start | bytes 3145736 | tf_op jit(solution)/shard_map/while/body/eval_jaxpr/ppermute | solution.py:10
  483.2 13.3 %copy-start.1 = (bf16[1024,1024]{1,0:T(8,128)(2,1)S(1)}, bf16[1024,1024]{1,0:T(8,128)(2,1)}, u32[]{:S(2)}) copy-start(bf16[1024,1024]{1,0:T(8,128)(2,1)} %get-tuple-element.351) | copy-start | bytes 6291460 | tf_op jit(solution)/shard_map/while
  506.4 17.2 %collective-permute-start = (bf16[1024,2,256]{2,0,1:T(8,128)(2,1)}, bf16[1024,2,256]{2,0,1:T(8,128)(2,1)S(1)}, u32[]{:S(2)}, u32[]{:S(2)}) collective-permute-start(bf16[1024,2,256]{2,0,1:T(8,128)(2,1)} %copy.31), channel_id=1, source_target_pairs={{0,4},{4,8},{8,12},{12,16},{16,20},{20,24},{24,28},{1,5},{5,9},{9,... | collective-permute-start | bytes 3145736 | tf_op jit(solution)/shard_map/while/body/eval_jaxpr/ppermute | solution.py:10
  512.3 13.3 %copy-start.1 = (bf16[1024,1024]{1,0:T(8,128)(2,1)S(1)}, bf16[1024,1024]{1,0:T(8,128)(2,1)}, u32[]{:S(2)}) copy-start(bf16[1024,1024]{1,0:T(8,128)(2,1)} %get-tuple-element.351) | copy-start | bytes 6291460 | tf_op jit(solution)/shard_map/while
  531.9 17.2 %collective-permute-start = (bf16[1024,2,256]{2,0,1:T(8,128)(2,1)}, bf16[1024,2,256]{2,0,1:T(8,128)(2,1)S(1)}, u32[]{:S(2)}, u32[]{:S(2)}) collective-permute-start(bf16[1024,2,256]{2,0,1:T(8,128)(2,1)} %copy.31), channel_id=1, source_target_pairs={{0,4},{4,8},{8,12},{12,16},{16,20},{20,24},{24,28},{1,5},{5,9},{9,... | collective-permute-start | bytes 3145736 | tf_op jit(solution)/shard_map/while/body/eval_jaxpr/ppermute | solution.py:10
  537.8 13.3 %copy-start.1 = (bf16[1024,1024]{1,0:T(8,128)(2,1)S(1)}, bf16[1024,1024]{1,0:T(8,128)(2,1)}, u32[]{:S(2)}) copy-start(bf16[1024,1024]{1,0:T(8,128)(2,1)} %get-tuple-element.351) | copy-start | bytes 6291460 | tf_op jit(solution)/shard_map/while
  557.4 17.2 %collective-permute-start = (bf16[1024,2,256]{2,0,1:T(8,128)(2,1)}, bf16[1024,2,256]{2,0,1:T(8,128)(2,1)S(1)}, u32[]{:S(2)}, u32[]{:S(2)}) collective-permute-start(bf16[1024,2,256]{2,0,1:T(8,128)(2,1)} %copy.31), channel_id=1, source_target_pairs={{0,4},{4,8},{8,12},{12,16},{16,20},{20,24},{24,28},{1,5},{5,9},{9,... | collective-permute-start | bytes 3145736 | tf_op jit(solution)/shard_map/while/body/eval_jaxpr/ppermute | solution.py:10
  563.3 13.3 %copy-start.1 = (bf16[1024,1024]{1,0:T(8,128)(2,1)S(1)}, bf16[1024,1024]{1,0:T(8,128)(2,1)}, u32[]{:S(2)}) copy-start(bf16[1024,1024]{1,0:T(8,128)(2,1)} %get-tuple-element.351) | copy-start | bytes 6291460 | tf_op jit(solution)/shard_map/while
Sparse Core Ops, SparseCore 0:
  43.8 86.7 all-gather.1
